TPU v7x, 32 devices: a whole 2x2x4 slice. The times are simulated.
32 devices in a mesh: sx: 8 (over z, core), sy: 4 (over y, x).
Axes of the slice: x: 2, y: 2, z: 4, core: 2. Of those that a mesh axis runs over, the one named last changes fastest.
Arguments:
- local_source: float32 [8, 4, 768, 256], P('sx', 'sy'), may hold values from -6 to 6
- schur: bfloat16 [8, 4, 768, 768], P('sx', 'sy')
- local_inverse: bfloat16 [8, 4, 768, 768], P('sx', 'sy')
- primal_basis: bfloat16 [8, 4, 768, 32], P('sx', 'sy'), may hold values from -0.21875 to 0.21875
- coarse_inverse: float32 [8, 4, 32, 32], P('sx', 'sy')
- primal_map: int32 [8, 4, 32], P('sx', 'sy'), may hold values from 0 to 255, as said below
- shared_count: int32 [8, 4, 8], P('sx', 'sy'), may hold values from 0 to 64, as said below
- row_order: int32 [8, 4, 768], P('sx', 'sy'), may hold values from 0 to 767, each once within a row
Outputs:
- solution: float32 [8, 4, 768, 256], P('sx', 'sy')
- residual: float32 [8, 4, 768, 256], P('sx', 'sy')
Inputs may be any that keep to these rules, and one draw needn't show every extreme that they name: shared_count[i, j, d] equals shared_count[i + a, j + b, 7 - d] for offset d = (a, b), and is 0 where (i + a, j + b) lies outside the 8 x 4 grid. A neighbour at offset (0, 1), (0, -1), (1, 0) or (-1, 0) inside the grid shares a quarter of 64 rows or more; a diagonal neighbour shares none or a quarter of 64 or more. Some pair shares exactly 64. primal_map[i, j, m] lies in block (i - 1) mod 8, i or (i + 1) mod 8, block b holding the coarse unknowns b * 32 to (b + 1) * 32 - 1. Each subdomain's row_order holds every row once.
All inputs are finite; a program needn't handle non-finite values.
Results may differ from a plain program's by a relative error of at most 0.0072.
Values sent between devices are 32-bit elements; how exact they have to be, the bound alone decides.
A program may use at most 64 MiB of HBM per device.

v0:
```python
import functools

import jax
import jax.numpy as jnp
from jax import lax
from jax.experimental import pallas as pl
from jax.experimental.pallas import tpu as pltpu
from jax.sharding import PartitionSpec as P

MROW = 64
ITERS = 3
CHUNKS = 2
MESH = pl.DeviceIdType.MESH

directions = ((-1, -1), (-1, 0), (-1, 1), (0, -1), (0, 1), (1, -1), (1, 0), (1, 1))
send_order = (0, 2, 5, 7, 3, 4, 1, 6)
ring = (-2, -1, 1, 2)
centre = 1.6
spread = 1.4
f32 = jnp.float32
bf16 = jnp.bfloat16
NN = (((1,), (0,)), ((), ()))
NT = (((1,), (1,)), ((), ()))
TN = (((0,), (0,)), ((), ()))


def mm(left, right, dims=NN):
    return lax.dot_general(left, right, dims, preferred_element_type=f32)


def exact(left, right, dims=NN):
    return lax.dot_general(left, right, dims, precision=lax.Precision.HIGHEST, preferred_element_type=f32)


def split(value):
    high = value.astype(bf16)
    return high, (value - high.astype(f32)).astype(bf16)


def spread_parts(one_hot, value):
    high, low = split(value)
    wide = value.shape[1]
    both = mm(one_hot[...], jnp.concatenate([high, low], axis=1))
    return both[:, :wide] + both[:, wide:]


def kernel(
    nx, ny,
    source, schur, inverse, basis, coarse, pmap, counts, order,
    sol_out, res_out,
    groups, perm, scatter, gather, schur_g, inverse_g, basis_g, weight, cmat,
    basis_n, local, direction, out_buf, in_buf, primal_in, maps, coarses,
    inverse_v, schur_v, load_sem, relay_buf, relay_send, relay_recv, out_send, out_recv, prim_send, prim_recv, meta_send, meta_recv,
):
    me_x, me_y = lax.axis_index("sx"), lax.axis_index("sy")
    rows, width = source.shape[2], source.shape[3]
    block = coarse.shape[2]
    modes = basis.shape[2]
    slots = 8 * MROW
    wide = width // CHUNKS

    def inside(d):
        a, b = directions[d]
        x, y = me_x + a, me_y + b
        return (x >= 0) & (x < nx) & (y >= 0) & (y < ny)

    def peer(d):
        a, b = directions[d]
        return (me_x + a, me_y + b)

    def ring_peer(s):
        return (lax.rem(me_x + s + nx, nx), me_y)

    loads = [
        pltpu.make_async_copy(inverse.at[0, 0], inverse_v, load_sem.at[0]),
        pltpu.make_async_copy(schur.at[0, 0], schur_v, load_sem.at[1]),
    ]
    for load in loads:
        load.start()
    barrier = pltpu.get_barrier_semaphore()
    total = jnp.int32(len(ring))
    for d in range(8):
        total = total + inside(d).astype(jnp.int32)

        @pl.when(inside(d))
        def _(d=d):
            pl.semaphore_signal(barrier, inc=1, device_id=peer(d), device_id_type=MESH)

    for s in ring:
        pl.semaphore_signal(barrier, inc=1, device_id=ring_peer(s), device_id_type=MESH)

    turn = ny // 2
    paired = {turn - 1: (ny - 1, 0), ny - 1: (turn - 1, turn), turn: (0, ny - 1), 0: (turn, turn - 1)}
    for mine, (straight, fan) in paired.items():
        at = me_y == mine
        total = total + at.astype(jnp.int32)

        @pl.when(at)
        def _(straight=straight):
            pl.semaphore_signal(barrier, inc=1, device_id=(me_x, straight), device_id_type=MESH)

        for a in (-1, 0, 1):
            valid = at & (me_x + a >= 0) & (me_x + a < nx)
            total = total + valid.astype(jnp.int32)

            @pl.when(valid)
            def _(fan=fan, a=a):
                pl.semaphore_signal(barrier, inc=1, device_id=(me_x + a, fan), device_id_type=MESH)

    k_of = lax.broadcasted_iota(jnp.int32, (MROW, rows), 0)
    p_of = lax.broadcasted_iota(jnp.int32, (MROW, rows), 1)
    start = jnp.int32(0)
    for d in range(8):
        count = counts[0, 0, d]
        hit = (p_of == k_of + start) & (k_of < count)
        groups[d * MROW:(d + 1) * MROW, :] = jnp.where(hit, 1.0, 0.0).astype(bf16)
        start = start + count
    r_of = lax.broadcasted_iota(jnp.int32, (rows, rows), 0)
    perm[...] = jnp.where(r_of == order[0], 1.0, 0.0).astype(bf16)
    gather[...] = mm(groups[...], perm[...], NT).astype(bf16)

    pl.semaphore_wait(barrier, total)

    def out_copy(stage, c, d):
        return pltpu.make_async_remote_copy(
            src_ref=out_buf.at[stage, c, pl.ds(d * MROW, MROW)],
            dst_ref=in_buf.at[stage, c, pl.ds((7 - d) * MROW, MROW)],
            send_sem=out_send.at[stage, c, d],
            recv_sem=out_recv.at[stage, c, 7 - d],
            device_id=peer(d),
            device_id_type=MESH,
        )

    def in_copy(stage, c, d):
        return pltpu.make_async_remote_copy(
            src_ref=out_buf.at[stage, c, pl.ds((7 - d) * MROW, MROW)],
            dst_ref=in_buf.at[stage, c, pl.ds(d * MROW, MROW)],
            send_sem=out_send.at[stage, c, 7 - d],
            recv_sem=out_recv.at[stage, c, d],
            device_id=peer(d),
            device_id_type=MESH,
        )

    def send_all(stage, c):
        for d in send_order:
            a, b = directions[d]
            direct = inside(d)
            if c == CHUNKS - 1 and b != 0:
                crossing = me_y == (turn - 1 if b > 0 else turn)

                @pl.when(inside(d) & crossing)
                def _(d=d, a=a, b=b):
                    pltpu.make_async_remote_copy(
                        src_ref=out_buf.at[stage, c, pl.ds(d * MROW, MROW)],
                        dst_ref=relay_buf.at[stage, a + 1],
                        send_sem=out_send.at[stage, c, d],
                        recv_sem=relay_recv.at[stage, a + 1],
                        device_id=(me_x, ny - 1 if b > 0 else 0),
                        device_id_type=MESH,
                    ).start()

                direct = direct & jnp.logical_not(crossing)

            @pl.when(direct)
            def _(d=d):
                out_copy(stage, c, d).start()

    def relay(stage, act):
        for b in (1, -1):
            for a in (-1, 0, 1):
                @pl.when((me_y == (ny - 1 if b > 0 else 0)) & (me_x + a >= 0) & (me_x + a < nx))
                def _(a=a, b=b):
                    d = directions.index((a, b))
                    act(pltpu.make_async_remote_copy(
                        src_ref=relay_buf.at[stage, a + 1],
                        dst_ref=in_buf.at[stage, CHUNKS - 1, pl.ds((7 - d) * MROW, MROW)],
                        send_sem=relay_send.at[stage, a + 1],
                        recv_sem=out_recv.at[stage, CHUNKS - 1, 7 - d],
                        device_id=(me_x + a, turn if b > 0 else turn - 1),
                        device_id_type=MESH,
                    ), pltpu.make_async_remote_copy(
                        src_ref=relay_buf.at[stage, a + 1],
                        dst_ref=relay_buf.at[stage, a + 1],
                        send_sem=relay_send.at[stage, a + 1],
                        recv_sem=relay_recv.at[stage, a + 1],
                        device_id=(me_x, turn - 1 if b > 0 else turn),
                        device_id_type=MESH,
                    ))

    def forward(onward, arriving):
        arriving.wait_recv()
        onward.start()

    def settle(onward, arriving):
        onward.wait_send()

    def receive(stage, c):
        for d in range(8):
            @pl.when(inside(d))
            def _(d=d):
                in_copy(stage, c, d).wait_recv()
        parts = []
        for d in range(8):
            part = in_buf[stage, c, d * MROW:(d + 1) * MROW, :]
            parts.append(jnp.where(inside(d), part, 0.0))
        return spread_parts(scatter, jnp.concatenate(parts, axis=0))

    def ring_copies(src, dst, slot_of, send, recv):
        copies = []
        for at, s in enumerate(ring):
            copies.append(pltpu.make_async_remote_copy(
                src_ref=src, dst_ref=dst(len(ring) - 1 - at), send_sem=send(at), recv_sem=recv(len(ring) - 1 - at),
                device_id=ring_peer(s), device_id_type=MESH,
            ))
        return copies

    def columns(c):
        return slice(c * wide, (c + 1) * wide)

    for c in range(CHUNKS):
        out_buf[0, c] = spread_parts(gather, source[0, 0, :, columns(c)])
        send_all(0, c)

    map_copies = ring_copies(
        pmap.at[0, 0], lambda t: maps.at[t], None, lambda t: meta_send.at[0, t], lambda t: meta_recv.at[0, t]
    )
    coarse_copies = ring_copies(
        coarse.at[0, 0], lambda t: coarses.at[t], None, lambda t: meta_send.at[1, t], lambda t: meta_recv.at[1, t]
    )
    for copy in map_copies + coarse_copies:
        copy.start()

    scatter[...] = mm(perm[...], groups[...], NT).astype(bf16)
    relay(0, forward)
    marks = mm(scatter[...], jnp.ones((slots, wide), bf16))
    weight[...] = 1.0 - 0.5 * marks
    half = (gather[...].astype(f32) * 0.5).astype(bf16)
    for load in loads:
        load.wait()
    inverse_g[...] = mm(half, inverse_v[...]).astype(bf16)
    basis_n[...] = basis[0, 0].astype(f32).T.astype(bf16)
    basis_g[...] = mm(half, basis_n[...]).astype(bf16)
    schur_g[...] = mm(gather[...], schur_v[...]).astype(bf16)

    for copy in map_copies + coarse_copies:
        copy.wait_recv()

    slot_iota = lax.broadcasted_iota(jnp.int32, (3 * block, modes), 0)

    def chooser(ids):
        relative = lax.rem(ids // block - me_x + 1 + 2 * nx, nx)
        target = relative * block + lax.rem(ids, block)
        return jnp.where(slot_iota == target, 1.0, 0.0).astype(f32)

    own = chooser(pmap[0, 0])
    blocks = (coarses[1], coarse[0, 0], coarses[2])

    chosen = jnp.concatenate([chooser(maps[t]) for t in range(len(ring))] + [own], axis=1)
    solved = [exact(blocks[t], chosen[t * block:(t + 1) * block, :]) for t in range(3)]
    cmat[...] = exact(own, jnp.concatenate(solved, axis=0), TN)

    def begin(step, c):
        stage = 1 + 2 * step
        scaled = (weight[...] * res_out[0, 0, :, columns(c)]).astype(bf16)
        primal_in[step, c, len(ring) * modes:(len(ring) + 1) * modes, :] = mm(basis[0, 0], scaled)
        for copy in prim_copies(primal_in, prim_send, prim_recv, ring_peer, step, c, modes):
            copy.start()
        out_buf[stage, c] = mm(inverse_g[...], scaled)
        local[c] = mm(inverse_v[...], scaled)

    for c in range(CHUNKS):
        res_out[0, 0, :, columns(c)] = source[0, 0, :, columns(c)] + receive(0, c)
        begin(0, c)

    sigma = centre / spread
    rho = 1.0 / sigma
    for step in range(ITERS):
        stage = 1 + 2 * step
        for c in range(CHUNKS):
            for copy in prim_copies(primal_in, prim_send, prim_recv, ring_peer, step, c, modes):
                copy.wait_recv()
            picked = exact(cmat[...], primal_in[step, c]).astype(bf16)
            out_buf[stage, c] = out_buf[stage, c] + mm(basis_g[...], picked)
            send_all(stage, c)
            local[c] = weight[...] * (local[c] + mm(basis_n[...], picked))
        relay(stage, forward)
        if step > 0:
            rho_new = 1.0 / (2.0 * sigma - rho)
            keep, gain = rho_new * rho, 2.0 * rho_new / spread
            rho = rho_new
        for c in range(CHUNKS):
            update = local[c] + receive(stage, c)
            if step == 0:
                moved = update / centre
                sol_out[0, 0, :, columns(c)] = moved
            else:
                moved = keep * direction[c] + gain * update
                sol_out[0, 0, :, columns(c)] = sol_out[0, 0, :, columns(c)] + moved
            direction[c] = moved
            rounded = moved.astype(bf16)
            out_buf[stage + 1, c] = mm(schur_g[...], rounded)
            send_all(stage + 1, c)
            local[c] = mm(schur_v[...], rounded)
        relay(stage + 1, forward)
        for c in range(CHUNKS):
            res_out[0, 0, :, columns(c)] = res_out[0, 0, :, columns(c)] - (local[c] + receive(stage + 1, c))
            if step + 1 < ITERS:
                begin(step + 1, c)

    for copy in map_copies + coarse_copies:
        copy.wait_send()
    for step in range(ITERS):
        for c in range(CHUNKS):
            for copy in prim_copies(primal_in, prim_send, prim_recv, ring_peer, step, c, modes):
                copy.wait_send()
    for stage in range(1 + 2 * ITERS):
        relay(stage, settle)
        for c in range(CHUNKS):
            for d in range(8):
                @pl.when(inside(d))
                def _(stage=stage, c=c, d=d):
                    out_copy(stage, c, d).wait_send()


def prim_copies(primal_in, send, recv, ring_peer, step, c, modes):
    last = len(ring) - 1
    return [
        pltpu.make_async_remote_copy(
            src_ref=primal_in.at[step, c, pl.ds(len(ring) * modes, modes)],
            dst_ref=primal_in.at[step, c, pl.ds((last - at) * modes, modes)],
            send_sem=send.at[step, c, at],
            recv_sem=recv.at[step, c, last - at],
            device_id=ring_peer(s),
            device_id_type=MESH,
        )
        for at, s in enumerate(ring)
    ]


def solution(mesh):
    nx, ny = mesh.shape["sx"], mesh.shape["sy"]

    def body(source, schur, inverse, basis, coarse, pmap, counts, order):
        rows, width = source.shape[2:]
        modes, block = basis.shape[3], coarse.shape[2]
        slots, wide, stages, links = 8 * MROW, width // CHUNKS, 1 + 2 * ITERS, len(ring)
        vmem = pl.BlockSpec(memory_space=pltpu.VMEM)
        hbm = pl.BlockSpec(memory_space=pl.ANY)
        smem = pl.BlockSpec(memory_space=pltpu.SMEM)
        dma = pltpu.SemaphoreType.DMA
        shape = jax.ShapeDtypeStruct(source.shape, f32)
        return pl.pallas_call(
            functools.partial(kernel, nx, ny),
            out_shape=(shape, shape),
            in_specs=[vmem, hbm, hbm, vmem, vmem, vmem, smem, vmem],
            out_specs=(vmem, vmem),
            scratch_shapes=[
                pltpu.VMEM((slots, rows), bf16),
                pltpu.VMEM((rows, rows), bf16),
                pltpu.VMEM((rows, slots), bf16),
                pltpu.VMEM((slots, rows), bf16),
                pltpu.VMEM((slots, rows), bf16),
                pltpu.VMEM((slots, rows), bf16),
                pltpu.VMEM((slots, modes), bf16),
                pltpu.VMEM((rows, wide), f32),
                pltpu.VMEM((modes, (links + 1) * modes), f32),
                pltpu.VMEM((rows, modes), bf16),
                pltpu.VMEM((CHUNKS, rows, wide), f32),
                pltpu.VMEM((CHUNKS, rows, wide), f32),
                pltpu.VMEM((stages, CHUNKS, slots, wide), f32),
                pltpu.VMEM((stages, CHUNKS, slots, wide), f32),
                pltpu.VMEM((ITERS, CHUNKS, (links + 1) * modes, wide), f32),
                pltpu.VMEM((links, 1, modes), jnp.int32),
                pltpu.VMEM((links, block, block), f32),
                pltpu.VMEM((rows, rows), bf16),
                pltpu.VMEM((rows, rows), bf16),
                dma((2,)),
                pltpu.VMEM((stages, 3, MROW, wide), f32),
                dma((stages, 3)),
                dma((stages, 3)),
                dma((stages, CHUNKS, 8)),
                dma((stages, CHUNKS, 8)),
                dma((ITERS, CHUNKS, links)),
                dma((ITERS, CHUNKS, links)),
                dma((2, links)),
                dma((2, links)),
            ],
            compiler_params=pltpu.CompilerParams(
                collective_id=0, has_side_effects=True, vmem_limit_bytes=56 * 1024 * 1024
            ),
        )(source, schur, inverse, jnp.swapaxes(basis, 2, 3), coarse, pmap[:, :, None, :], counts, order)

    placed = (P("sx", "sy", None, None),) * 5 + (P("sx", "sy", None),) * 3
    return jax.shard_map(
        body,
        mesh=mesh,
        in_specs=placed,
        out_specs=(P("sx", "sy", None, None), P("sx", "sy", None, None)),
        check_vma=False,
    )
```

profile of v0, /device:TPU:13, one launch (start us, length us, event | category | flops | bytes accessed | tf_op | source)
XLA Modules:
  0.0 82.7 jit_solution(3561836783234377311)
XLA Ops:
  0.6 79.1 %shard_map.95 = (f32[1,1,768,256]{3,2,1,0:T(8,128)}, f32[1,1,768,256]{3,2,1,0:T(8,128)}) custom-call(f32[1,1,768,256]{3,2,1,0:T(8,128)} %source.1, bf16[1,1,768,768]{3,2,1,0:T(8,128)(2,1)} %schur.1, bf16[1,1,768,768]{3,2,1,0:T(8,128)(2,1)} %inverse.1, bf16[1,1,32,768]{3,2,1,0:T(8,128)(2,1)} %bitcast.2, f32[1,1,32,32]{3,2,1,0:T(8,128)} %coarse.1, ...), custom_call_target="tpu_custom_call" | custom-call | tf_op jit(solution)/shard_map/pallas_call | solution.py:352
  79.7 0.0 copy-start
  79.7 2.1 %copy.12 = f32[1,1,768,256]{3,2,1,0:T(8,128)} copy(f32[1,1,768,256]{3,2,1,0:T(8,128)} %get-tuple-element.4) | data formatting | bytes 1572864
  81.9 0.0 copy-done
  81.9 0.9 %copy.13 = f32[1,1,768,256]{3,2,1,0:T(8,128)} copy(f32[1,1,768,256]{3,2,1,0:T(8,128)S(1)} %copy-done) | data formatting | bytes 1572864
Async XLA Ops:
  79.7 2.1 %copy-start = (f32[1,1,768,256]{3,2,1,0:T(8,128)S(1)}, f32[1,1,768,256]{3,2,1,0:T(8,128)}, u32[]{:S(2)}) copy-start(f32[1,1,768,256]{3,2,1,0:T(8,128)} %get-tuple-element.5) | copy-start | bytes 2359300
where the time goes:
time: 82.9 us; the launch traced here: 82.7 us
  Pallas kernels  79.1 us (95%)
  local copies, waits for them, and re-layouts  3.02 us (4%)
    pallas_call x1, Pallas kernels, body(): pl.pallas_call(functools.partial(kernel, nx, ny), out_shape=(shape, shape...  79.1 us
    unnamed x4, local copies, waits for them, and re-layouts  3.02 us

commit v1 on v0

v1 whole, which is shorter than its diff:
```python
import functools

import jax
import jax.numpy as jnp
from jax import lax
from jax.experimental import pallas as pl
from jax.experimental.pallas import tpu as pltpu
from jax.sharding import PartitionSpec as P

MROW = 64
ITERS = 3
CHUNKS = 4
LANES = 128
MESH = pl.DeviceIdType.MESH

directions = ((-1, -1), (-1, 0), (-1, 1), (0, -1), (0, 1), (1, -1), (1, 0), (1, 1))
send_order = (0, 2, 5, 7, 3, 4, 1, 6)
ring = (-2, -1, 1, 2)
centre = 1.6
spread = 1.4
f32 = jnp.float32
bf16 = jnp.bfloat16
NN = (((1,), (0,)), ((), ()))
TN = (((0,), (0,)), ((), ()))


def mm(left, right, dims=NN):
    return lax.dot_general(left, right, dims, preferred_element_type=f32)


def exact(left, right, dims=NN):
    return lax.dot_general(left, right, dims, precision=lax.Precision.HIGHEST, preferred_element_type=f32)


def split(value):
    high = value.astype(bf16)
    return high, (value - high.astype(f32)).astype(bf16)


def select_rows(value, one_hot):
    count = value.shape[0]
    both = mm(jnp.concatenate(split(value), axis=0), one_hot)
    return both[:count] + both[count:]


def iota(shape, axis):
    return lax.broadcasted_iota(jnp.int32, shape, axis)


def kernel(
    nx, ny,
    source, schur, inverse, basis, coarse, pmap, counts, order,
    sol_out, res_out,
    source_v, inverse_v, schur_v, gather, scatter, inverse_g, inverse_w, schur_g, schur_w, basis_q, picked_g, picked_w,
    cmat, weight, res, sol, direction, local, shared, out_buf, in_buf, prim_buf, maps, coarses,
    load_sem, out_send, out_recv, prim_send, prim_recv, meta_send, meta_recv,
):
    me_x, me_y = lax.axis_index("sx"), lax.axis_index("sy")
    rows, width = source.shape[2], source.shape[3]
    block = coarse.shape[2]
    modes = basis.shape[2]
    slots = 8 * MROW
    links = len(ring)
    stages = 1 + 2 * ITERS
    wide = width // CHUNKS
    half = wide // 2
    parts = LANES // modes
    quarter = wide // parts

    def inside(d):
        a, b = directions[d]
        x, y = me_x + a, me_y + b
        return (x >= 0) & (x < nx) & (y >= 0) & (y < ny)

    def peer(d):
        a, b = directions[d]
        return (me_x + a, me_y + b)

    def ring_peer(s):
        return (lax.rem(me_x + s + nx, nx), me_y)

    load_source = pltpu.make_async_copy(source.at[0, 0], source_v, load_sem.at[0])
    load_inverse = pltpu.make_async_copy(inverse.at[0, 0], inverse_v, load_sem.at[1])
    load_schur = pltpu.make_async_copy(schur.at[0, 0], schur_v, load_sem.at[2])
    load_source.start()
    load_inverse.start()
    load_schur.start()

    barrier = pltpu.get_barrier_semaphore()
    total = jnp.int32(links)
    for d in range(8):
        total = total + inside(d).astype(jnp.int32)

        @pl.when(inside(d))
        def _(d=d):
            pl.semaphore_signal(barrier, inc=1, device_id=peer(d), device_id_type=MESH)

    for s in ring:
        pl.semaphore_signal(barrier, inc=1, device_id=ring_peer(s), device_id_type=MESH)

    slot = iota((1, slots), 1)
    begins = jnp.zeros((1, slots), jnp.int32)
    sizes = jnp.zeros((1, slots), jnp.int32)
    start = jnp.int32(0)
    for d in range(8):
        count = counts[0, 0, d]
        mine = slot // MROW == d
        begins = jnp.where(mine, start, begins)
        sizes = jnp.where(mine, count, sizes)
        start = start + count
    place = lax.rem(slot, MROW)
    position = jnp.where(place < sizes, begins + place, -1)
    row_of = iota((rows, slots), 0)
    scatter[...] = jnp.where(row_of == position, 1.0, 0.0).astype(bf16)
    digit = iota((16, rows), 0)
    ids = order[0]
    digits = jnp.where(digit == 0, ids // 256, jnp.where(digit == 1, lax.rem(ids, 256), 1))
    found = mm(digits.astype(f32).astype(bf16), scatter[...])
    target = jnp.where(found[2:3] > 0.5, 256.0 * found[0:1] + found[1:2], -1.0)
    scatter[...] = jnp.where(row_of == target.astype(jnp.int32), 1.0, 0.0).astype(bf16)

    low_lanes = iota((half, LANES), 1) < MROW

    def out_copy(stage, c, d):
        return pltpu.make_async_remote_copy(
            src_ref=out_buf.at[d, stage, c],
            dst_ref=in_buf.at[7 - d, stage, c],
            send_sem=out_send.at[d],
            recv_sem=out_recv.at[stage, c, 7 - d],
            device_id=peer(d),
            device_id_type=MESH,
        )

    def in_copy(stage, c, d):
        return pltpu.make_async_remote_copy(
            src_ref=out_buf.at[7 - d, stage, c],
            dst_ref=in_buf.at[d, stage, c],
            send_sem=out_send.at[7 - d],
            recv_sem=out_recv.at[stage, c, d],
            device_id=peer(d),
            device_id_type=MESH,
        )

    def pack(stage, c, value):
        for t in range(slots // LANES):
            tile = value[:, t * LANES:(t + 1) * LANES]
            top, low = tile[:half], tile[half:]
            out_buf[2 * t, stage, c] = jnp.where(low_lanes, top, pltpu.roll(low, MROW, 1))
            out_buf[2 * t + 1, stage, c] = jnp.where(low_lanes, pltpu.roll(top, MROW, 1), low)

    def send_all(stage, c):
        for d in send_order:
            @pl.when(inside(d))
            def _(d=d):
                out_copy(stage, c, d).start()

    def receive(stage, c):
        for d in range(8):
            @pl.when(inside(d))
            def _(d=d):
                in_copy(stage, c, d).wait_recv()
        tops, lows = [], []
        for t in range(slots // LANES):
            first, second = in_buf[2 * t, stage, c], in_buf[2 * t + 1, stage, c]
            tops.append(jnp.where(low_lanes, first, pltpu.roll(second, MROW, 1)))
            lows.append(jnp.where(low_lanes, pltpu.roll(first, MROW, 1), second))
        value = jnp.concatenate([jnp.concatenate(tops, axis=1), jnp.concatenate(lows, axis=1)], axis=0)
        return select_rows(value, gather[...])

    def ring_copies(src, dst, send, recv):
        return [
            pltpu.make_async_remote_copy(
                src_ref=src, dst_ref=dst(links - 1 - at), send_sem=send(at), recv_sem=recv(links - 1 - at),
                device_id=ring_peer(s), device_id_type=MESH,
            )
            for at, s in enumerate(ring)
        ]

    def prim_copies(step, c):
        return ring_copies(
            prim_buf.at[links, step, c], lambda t: prim_buf.at[t, step, c],
            lambda t: prim_send.at[t], lambda t: prim_recv.at[step, c, t],
        )

    def chunk(c):
        return slice(c * wide, (c + 1) * wide)

    for d in range(8):
        @pl.when(jnp.logical_not(inside(d)))
        def _(d=d):
            in_buf[d] = jnp.zeros(in_buf.shape[1:], f32)

    load_source.wait()
    for at in range(width // LANES):
        res[at * LANES:(at + 1) * LANES, :] = source_v[:, at * LANES:(at + 1) * LANES].T
    for c in range(CHUNKS):
        pack(0, c, select_rows(res[chunk(c), :], scatter[...]))
        if c == 0:
            pl.semaphore_wait(barrier, total)
        send_all(0, c)

    map_copies = ring_copies(
        pmap.at[0, 0], lambda t: maps.at[t], lambda t: meta_send.at[0, t], lambda t: meta_recv.at[0, t]
    )
    coarse_copies = ring_copies(
        coarse.at[0, 0], lambda t: coarses.at[t], lambda t: meta_send.at[1, t], lambda t: meta_recv.at[1, t]
    )
    for copy in map_copies + coarse_copies:
        copy.start()

    column = jnp.broadcast_to(target, (8, slots)).T[:, 0:1].astype(jnp.int32)
    gather[...] = jnp.where(iota((slots, rows), 1) == column, 1.0, 0.0).astype(bf16)
    marks = mm(jnp.ones((16, slots), bf16), gather[...])
    weight[...] = 1.0 - 0.5 * marks[:8]
    scale = weight[0:1, :]
    halved = (scatter[...].astype(f32) * 0.5).astype(bf16)
    basis_t = basis[0, 0]
    basis_q[...] = jnp.concatenate([basis_t.astype(f32)] * parts, axis=0).T.astype(bf16)
    picked_g[...] = jnp.concatenate([mm(basis_t, halved)] * parts, axis=0).astype(bf16)
    picked_w[...] = jnp.concatenate([basis_t.astype(f32) * scale] * parts, axis=0).astype(bf16)
    load_inverse.wait()
    inverse_w[...] = inverse_v[...].T
    inverse_g[...] = mm(inverse_w[...], halved).astype(bf16)
    inverse_w[...] = (inverse_w[...].astype(f32) * scale).astype(bf16)
    load_schur.wait()
    schur_w[...] = schur_v[...].T
    schur_g[...] = mm(schur_w[...], scatter[...]).astype(bf16)

    for copy in map_copies + coarse_copies:
        copy.wait_recv()

    slot_iota = iota((3 * block, modes), 0)

    def chooser(ids):
        relative = lax.rem(ids // block - me_x + 1 + 2 * nx, nx)
        place = relative * block + lax.rem(ids, block)
        return jnp.where(slot_iota == place, 1.0, 0.0).astype(f32)

    own = chooser(pmap[0, 0])
    blocks = (coarses[1], coarse[0, 0], coarses[2])
    chosen = jnp.concatenate([chooser(maps[t]) for t in range(links)] + [own], axis=1)
    solved = jnp.concatenate(
        [exact(blocks[t], chosen[t * block:(t + 1) * block, :]) for t in range(3)], axis=0
    )
    mapped = exact(solved, jnp.concatenate([own] * parts, axis=1), TN)
    same = iota((LANES, LANES), 0) // modes == iota((LANES, LANES), 1) // modes
    for t in range(links + 1):
        tiled = jnp.where(same, jnp.concatenate([mapped[t * modes:(t + 1) * modes]] * parts, axis=0), 0.0)
        high, low = split(tiled)
        cmat[t * LANES:(t + 1) * LANES, :LANES] = high
        cmat[t * LANES:(t + 1) * LANES, LANES:] = low

    part_of = iota((quarter, LANES), 1) // modes

    def begin(step, c):
        scaled = (weight[0:1, :] * res[chunk(c), :]).astype(bf16)
        primal = mm(scaled, basis_q[...])
        packed = primal[:quarter]
        for q in range(1, parts):
            packed = jnp.where(part_of == q, primal[q * quarter:(q + 1) * quarter], packed)
        prim_buf[links, step, c] = packed
        for copy in prim_copies(step, c):
            copy.start()
        shared[chunk(c), :] = mm(scaled, inverse_g[...])
        local[chunk(c), :] = mm(scaled, inverse_w[...])

    def finish(step, c):
        for copy in prim_copies(step, c):
            copy.wait_recv()
        primal = jnp.concatenate([prim_buf[t, step, c] for t in range(links + 1)], axis=1)
        both = mm(jnp.concatenate(split(primal), axis=0), cmat[...])
        packed = both[:quarter, :LANES] + (both[quarter:, :LANES] + both[:quarter, LANES:])
        picked = jnp.concatenate(
            [jnp.where(part_of == q, packed, 0.0) for q in range(parts)], axis=0
        ).astype(bf16)
        pack(1 + 2 * step, c, shared[chunk(c), :] + mm(picked, picked_g[...]))
        send_all(1 + 2 * step, c)
        local[chunk(c), :] = local[chunk(c), :] + mm(picked, picked_w[...])

    for c in range(CHUNKS):
        res[chunk(c), :] = res[chunk(c), :] + receive(0, c)
        begin(0, c)

    sigma = centre / spread
    rho = 1.0 / sigma
    for step in range(ITERS):
        stage = 1 + 2 * step
        for c in range(CHUNKS):
            finish(step, c)
        if step > 0:
            rho_new = 1.0 / (2.0 * sigma - rho)
            keep, gain = rho_new * rho, 2.0 * rho_new / spread
            rho = rho_new
        for c in range(CHUNKS):
            update = local[chunk(c), :] + receive(stage, c)
            if step == 0:
                moved = update / centre
                sol[chunk(c), :] = moved
            else:
                moved = keep * direction[chunk(c), :] + gain * update
                sol[chunk(c), :] = sol[chunk(c), :] + moved
            direction[chunk(c), :] = moved
            rounded = moved.astype(bf16)
            pack(stage + 1, c, mm(rounded, schur_g[...]))
            send_all(stage + 1, c)
            local[chunk(c), :] = mm(rounded, schur_w[...])
        if step + 1 == ITERS:
            for at in range(width // LANES):
                sol_out[0, 0, :, at * LANES:(at + 1) * LANES] = sol[at * LANES:(at + 1) * LANES, :].T
        for c in range(CHUNKS):
            res[chunk(c), :] = res[chunk(c), :] - (local[chunk(c), :] + receive(stage + 1, c))
            if step + 1 < ITERS:
                begin(step + 1, c)
    for at in range(width // LANES):
        res_out[0, 0, :, at * LANES:(at + 1) * LANES] = res[at * LANES:(at + 1) * LANES, :].T

    for copy in map_copies + coarse_copies:
        copy.wait_send()
    for at, s in enumerate(ring):
        pltpu.make_async_remote_copy(
            src_ref=prim_buf.at[links], dst_ref=prim_buf.at[links - 1 - at],
            send_sem=prim_send.at[at], recv_sem=prim_recv.at[0, 0, 0],
            device_id=ring_peer(s), device_id_type=MESH,
        ).wait_send()
    for d in range(8):
        @pl.when(inside(d))
        def _(d=d):
            pltpu.make_async_remote_copy(
                src_ref=out_buf.at[d], dst_ref=in_buf.at[7 - d],
                send_sem=out_send.at[d], recv_sem=out_recv.at[0, 0, 0],
                device_id=peer(d), device_id_type=MESH,
            ).wait_send()


def solution(mesh):
    nx, ny = mesh.shape["sx"], mesh.shape["sy"]

    def body(source, schur, inverse, basis, coarse, pmap, counts, order):
        rows, width = source.shape[2:]
        modes, block = basis.shape[3], coarse.shape[2]
        slots, wide, stages, links = 8 * MROW, width // CHUNKS, 1 + 2 * ITERS, len(ring)
        half, quarter = wide // 2, wide * modes // LANES
        vmem = pl.BlockSpec(memory_space=pltpu.VMEM)
        hbm = pl.BlockSpec(memory_space=pl.ANY)
        smem = pl.BlockSpec(memory_space=pltpu.SMEM)
        dma = pltpu.SemaphoreType.DMA
        shape = jax.ShapeDtypeStruct(source.shape, f32)
        return pl.pallas_call(
            functools.partial(kernel, nx, ny),
            out_shape=(shape, shape),
            in_specs=[hbm, hbm, hbm, vmem, vmem, vmem, smem, vmem],
            out_specs=(vmem, vmem),
            scratch_shapes=[
                pltpu.VMEM((rows, width), f32),
                pltpu.VMEM((rows, rows), bf16),
                pltpu.VMEM((rows, rows), bf16),
                pltpu.VMEM((slots, rows), bf16),
                pltpu.VMEM((rows, slots), bf16),
                pltpu.VMEM((rows, slots), bf16),
                pltpu.VMEM((rows, rows), bf16),
                pltpu.VMEM((rows, slots), bf16),
                pltpu.VMEM((rows, rows), bf16),
                pltpu.VMEM((rows, LANES), bf16),
                pltpu.VMEM((LANES, slots), bf16),
                pltpu.VMEM((LANES, rows), bf16),
                pltpu.VMEM(((links + 1) * LANES, 2 * LANES), bf16),
                pltpu.VMEM((8, rows), f32),
                pltpu.VMEM((width, rows), f32),
                pltpu.VMEM((width, rows), f32),
                pltpu.VMEM((width, rows), f32),
                pltpu.VMEM((width, rows), f32),
                pltpu.VMEM((width, slots), f32),
                pltpu.VMEM((8, stages, CHUNKS, half, LANES), f32),
                pltpu.VMEM((8, stages, CHUNKS, half, LANES), f32),
                pltpu.VMEM((links + 1, ITERS, CHUNKS, quarter, LANES), f32),
                pltpu.VMEM((links, 1, modes), jnp.int32),
                pltpu.VMEM((links, block, block), f32),
                dma((3,)),
                dma((8,)),
                dma((stages, CHUNKS, 8)),
                dma((links,)),
                dma((ITERS, CHUNKS, links)),
                dma((2, links)),
                dma((2, links)),
            ],
            compiler_params=pltpu.CompilerParams(
                collective_id=0, has_side_effects=True, vmem_limit_bytes=56 * 1024 * 1024
            ),
        )(source, schur, inverse, jnp.swapaxes(basis, 2, 3), coarse, pmap[:, :, None, :], counts, order)

    placed = (P("sx", "sy", None, None),) * 5 + (P("sx", "sy", None),) * 3
    return jax.shard_map(
        body,
        mesh=mesh,
        in_specs=placed,
        out_specs=(P("sx", "sy", None, None), P("sx", "sy", None, None)),
        check_vma=False,
    )
```

time: 82.9 us -> 81.4 us (0.982)
  Pallas kernels: 79.1 us -> 77.1 us
    pallas_call x1, Pallas kernels: 79.1 us -> 77.1 us  [body(): pl.pallas_call(functools.partial(kernel, nx, ny), out_shape=(shape, shape...]
where the time goes in v1:
time: 81.4 us; the launch traced here: 80.8 us
  Pallas kernels  77.1 us (95%)
  local copies, waits for them, and re-layouts  3.02 us (4%)
    pallas_call x1, Pallas kernels, body(): pl.pallas_call(functools.partial(kernel, nx, ny), out_shape=(shape, shape...  77.1 us
    unnamed x4, local copies, waits for them, and re-layouts  3.02 us

profile of v1, /device:TPU:13, one launch (start us, length us, event | category | flops | bytes accessed | tf_op | source)
XLA Modules:
  0.0 80.8 jit_solution(10027726803656007672)
XLA Ops:
  0.6 77.1 %shard_map.95 = (f32[1,1,768,256]{3,2,1,0:T(8,128)}, f32[1,1,768,256]{3,2,1,0:T(8,128)}) custom-call(f32[1,1,768,256]{3,2,1,0:T(8,128)} %source.1, bf16[1,1,768,768]{3,2,1,0:T(8,128)(2,1)} %schur.1, bf16[1,1,768,768]{3,2,1,0:T(8,128)(2,1)} %inverse.1, bf16[1,1,32,768]{3,2,1,0:T(8,128)(2,1)} %bitcast.2, f32[1,1,32,32]{3,2,1,0:T(8,128)} %coarse.1, ...), custom_call_target="tpu_custom_call" | custom-call | tf_op jit(solution)/shard_map/pallas_call | solution.py:348
  77.7 0.0 copy-start
  77.7 2.1 %copy.12 = f32[1,1,768,256]{3,2,1,0:T(8,128)} copy(f32[1,1,768,256]{3,2,1,0:T(8,128)} %get-tuple-element.4) | data formatting | bytes 1572864
  79.9 0.0 copy-done
  79.9 0.9 %copy.13 = f32[1,1,768,256]{3,2,1,0:T(8,128)} copy(f32[1,1,768,256]{3,2,1,0:T(8,128)S(1)} %copy-done) | data formatting | bytes 1572864
Async XLA Ops:
  77.7 2.1 %copy-start = (f32[1,1,768,256]{3,2,1,0:T(8,128)S(1)}, f32[1,1,768,256]{3,2,1,0:T(8,128)}, u32[]{:S(2)}) copy-start(f32[1,1,768,256]{3,2,1,0:T(8,128)} %get-tuple-element.5) | copy-start | bytes 2359300

commit v2 on v1

--- a/solution.py
+++ b/solution.py
@@ -10,6 +10,7 @@
 MROW = 64
 ITERS = 3
 CHUNKS = 4
+RELAYED = ((), (-1, 0, 1), (0,), ())
 LANES = 128
 MESH = pl.DeviceIdType.MESH
 
@@ -52,8 +53,8 @@
     source, schur, inverse, basis, coarse, pmap, counts, order,
     sol_out, res_out,
     source_v, inverse_v, schur_v, gather, scatter, inverse_g, inverse_w, schur_g, schur_w, basis_q, picked_g, picked_w,
-    cmat, weight, res, sol, direction, local, shared, out_buf, in_buf, prim_buf, maps, coarses,
-    load_sem, out_send, out_recv, prim_send, prim_recv, meta_send, meta_recv,
+    cmat, weight, res, sol, direction, local, shared, operand, picks, out_buf, in_buf, relay_buf, prim_buf, maps, coarses,
+    load_sem, out_send, out_recv, relay_send, relay_recv, prim_send, prim_recv, meta_send, meta_recv,
 ):
     me_x, me_y = lax.axis_index("sx"), lax.axis_index("sy")
     rows, width = source.shape[2], source.shape[3]
@@ -97,6 +98,24 @@
 
     for s in ring:
         pl.semaphore_signal(barrier, inc=1, device_id=ring_peer(s), device_id_type=MESH)
+
+    turn = ny // 2
+    paired = {turn - 1: (ny - 1, 0), ny - 1: (turn - 1, turn), turn: (0, ny - 1), 0: (turn, turn - 1)}
+    for mine, (straight, fan) in paired.items():
+        at = me_y == mine
+        total = total + at.astype(jnp.int32)
+
+        @pl.when(at)
+        def _(straight=straight):
+            pl.semaphore_signal(barrier, inc=1, device_id=(me_x, straight), device_id_type=MESH)
+
+        for a in (-1, 0, 1):
+            valid = at & (me_x + a >= 0) & (me_x + a < nx)
+            total = total + valid.astype(jnp.int32)
+
+            @pl.when(valid)
+            def _(fan=fan, a=a):
+                pl.semaphore_signal(barrier, inc=1, device_id=(me_x + a, fan), device_id_type=MESH)
 
     slot = iota((1, slots), 1)
     begins = jnp.zeros((1, slots), jnp.int32)
@@ -126,7 +145,7 @@
             src_ref=out_buf.at[d, stage, c],
             dst_ref=in_buf.at[7 - d, stage, c],
             send_sem=out_send.at[d],
-            recv_sem=out_recv.at[stage, c, 7 - d],
+            recv_sem=out_recv.at[stage % 2, c, 7 - d],
             device_id=peer(d),
             device_id_type=MESH,
         )
@@ -136,7 +155,7 @@
             src_ref=out_buf.at[7 - d, stage, c],
             dst_ref=in_buf.at[d, stage, c],
             send_sem=out_send.at[7 - d],
-            recv_sem=out_recv.at[stage, c, d],
+            recv_sem=out_recv.at[stage % 2, c, d],
             device_id=peer(d),
             device_id_type=MESH,
         )
@@ -150,15 +169,68 @@
 
     def send_all(stage, c):
         for d in send_order:
-            @pl.when(inside(d))
+            a, b = directions[d]
+            direct = inside(d)
+            if a in RELAYED[c] and b != 0:
+                crossing = me_y == (turn - 1 if b > 0 else turn)
+
+                @pl.when(inside(d) & crossing)
+                def _(d=d, a=a, b=b):
+                    pltpu.make_async_remote_copy(
+                        src_ref=out_buf.at[d, stage, c],
+                        dst_ref=relay_buf.at[a + 1, stage, c],
+                        send_sem=out_send.at[d],
+                        recv_sem=relay_recv.at[a + 1, stage % 2, c],
+                        device_id=(me_x, ny - 1 if b > 0 else 0),
+                        device_id_type=MESH,
+                    ).start()
+
+                direct = direct & jnp.logical_not(crossing)
+
+            @pl.when(direct)
             def _(d=d):
                 out_copy(stage, c, d).start()
 
-    def receive(stage, c):
+    def relay(stage, c):
+        if not RELAYED[c]:
+            return
+        for b in (1, -1):
+            @pl.when(me_y == (ny - 1 if b > 0 else 0))
+            def _(b=b):
+                for a in RELAYED[c]:
+                    @pl.when((me_x + a >= 0) & (me_x + a < nx))
+                    def _(a=a):
+                        slot = 7 - directions.index((a, b))
+                        pltpu.make_async_remote_copy(
+                            src_ref=relay_buf.at[a + 1, stage, c],
+                            dst_ref=relay_buf.at[a + 1, stage, c],
+                            send_sem=relay_send.at[a + 1],
+                            recv_sem=relay_recv.at[a + 1, stage % 2, c],
+                            device_id=(me_x, turn - 1 if b > 0 else turn),
+                            device_id_type=MESH,
+                        ).wait_recv()
+                        pltpu.make_async_remote_copy(
+                            src_ref=relay_buf.at[a + 1, stage, c],
+                            dst_ref=in_buf.at[slot, stage, c],
+                            send_sem=relay_send.at[a + 1],
+                            recv_sem=out_recv.at[stage % 2, c, slot],
+                            device_id=(me_x + a, turn if b > 0 else turn - 1),
+                            device_id_type=MESH,
+                        ).start()
+
+
+    def wait_all(stage, c):
         for d in range(8):
             @pl.when(inside(d))
             def _(d=d):
                 in_copy(stage, c, d).wait_recv()
+
+    def relay_all(stage):
+        for c in range(CHUNKS):
+            relay(stage, c)
+
+    def receive(stage, c):
+        wait_all(stage, c)
         tops, lows = [], []
         for t in range(slots // LANES):
             first, second = in_buf[2 * t, stage, c], in_buf[2 * t + 1, stage, c]
@@ -190,6 +262,12 @@
         def _(d=d):
             in_buf[d] = jnp.zeros(in_buf.shape[1:], f32)
 
+    map_copies = ring_copies(
+        pmap.at[0, 0], lambda t: maps.at[t], lambda t: meta_send.at[0, t], lambda t: meta_recv.at[0, t]
+    )
+    coarse_copies = ring_copies(
+        coarse.at[0, 0], lambda t: coarses.at[t], lambda t: meta_send.at[1, t], lambda t: meta_recv.at[1, t]
+    )
     load_source.wait()
     for at in range(width // LANES):
         res[at * LANES:(at + 1) * LANES, :] = source_v[:, at * LANES:(at + 1) * LANES].T
@@ -197,16 +275,9 @@
         pack(0, c, select_rows(res[chunk(c), :], scatter[...]))
         if c == 0:
             pl.semaphore_wait(barrier, total)
+            for copy in map_copies + coarse_copies:
+                copy.start()
         send_all(0, c)
-
-    map_copies = ring_copies(
-        pmap.at[0, 0], lambda t: maps.at[t], lambda t: meta_send.at[0, t], lambda t: meta_recv.at[0, t]
-    )
-    coarse_copies = ring_copies(
-        coarse.at[0, 0], lambda t: coarses.at[t], lambda t: meta_send.at[1, t], lambda t: meta_recv.at[1, t]
-    )
-    for copy in map_copies + coarse_copies:
-        copy.start()
 
     column = jnp.broadcast_to(target, (8, slots)).T[:, 0:1].astype(jnp.int32)
     gather[...] = jnp.where(iota((slots, rows), 1) == column, 1.0, 0.0).astype(bf16)
@@ -218,10 +289,41 @@
     basis_q[...] = jnp.concatenate([basis_t.astype(f32)] * parts, axis=0).T.astype(bf16)
     picked_g[...] = jnp.concatenate([mm(basis_t, halved)] * parts, axis=0).astype(bf16)
     picked_w[...] = jnp.concatenate([basis_t.astype(f32) * scale] * parts, axis=0).astype(bf16)
+    relay_all(0)
     load_inverse.wait()
     inverse_w[...] = inverse_v[...].T
     inverse_g[...] = mm(inverse_w[...], halved).astype(bf16)
     inverse_w[...] = (inverse_w[...].astype(f32) * scale).astype(bf16)
+    part_of = iota((quarter, LANES), 1) // modes
+
+    def begin(step, c):
+        scaled = (weight[0:1, :] * res[chunk(c), :]).astype(bf16)
+        primal = mm(scaled, basis_q[...])
+        packed = primal[:quarter]
+        for q in range(1, parts):
+            packed = jnp.where(part_of == q, primal[q * quarter:(q + 1) * quarter], packed)
+        prim_buf[links, step, c] = packed
+        for copy in prim_copies(step, c):
+            copy.start()
+        shared[chunk(c), :] = mm(scaled, inverse_g[...])
+        operand[chunk(c), :] = scaled
+
+    def wait_prim(step, c):
+        for copy in prim_copies(step, c):
+            copy.wait_recv()
+
+    def finish(step, c):
+        wait_prim(step, c)
+        primal = jnp.concatenate([prim_buf[t, step, c] for t in range(links + 1)], axis=1)
+        both = mm(jnp.concatenate(split(primal), axis=0), cmat[...])
+        packed = both[:quarter, :LANES] + (both[quarter:, :LANES] + both[:quarter, LANES:])
+        picked = jnp.concatenate(
+            [jnp.where(part_of == q, packed, 0.0) for q in range(parts)], axis=0
+        ).astype(bf16)
+        pack(1 + 2 * step, c, shared[chunk(c), :] + mm(picked, picked_g[...]))
+        send_all(1 + 2 * step, c)
+        picks[chunk(c), :] = picked
+
     load_schur.wait()
     schur_w[...] = schur_v[...].T
     schur_g[...] = mm(schur_w[...], scatter[...]).astype(bf16)
@@ -250,33 +352,6 @@
         cmat[t * LANES:(t + 1) * LANES, :LANES] = high
         cmat[t * LANES:(t + 1) * LANES, LANES:] = low
 
-    part_of = iota((quarter, LANES), 1) // modes
-
-    def begin(step, c):
-        scaled = (weight[0:1, :] * res[chunk(c), :]).astype(bf16)
-        primal = mm(scaled, basis_q[...])
-        packed = primal[:quarter]
-        for q in range(1, parts):
-            packed = jnp.where(part_of == q, primal[q * quarter:(q + 1) * quarter], packed)
-        prim_buf[links, step, c] = packed
-        for copy in prim_copies(step, c):
-            copy.start()
-        shared[chunk(c), :] = mm(scaled, inverse_g[...])
-        local[chunk(c), :] = mm(scaled, inverse_w[...])
-
-    def finish(step, c):
-        for copy in prim_copies(step, c):
-            copy.wait_recv()
-        primal = jnp.concatenate([prim_buf[t, step, c] for t in range(links + 1)], axis=1)
-        both = mm(jnp.concatenate(split(primal), axis=0), cmat[...])
-        packed = both[:quarter, :LANES] + (both[quarter:, :LANES] + both[:quarter, LANES:])
-        picked = jnp.concatenate(
-            [jnp.where(part_of == q, packed, 0.0) for q in range(parts)], axis=0
-        ).astype(bf16)
-        pack(1 + 2 * step, c, shared[chunk(c), :] + mm(picked, picked_g[...]))
-        send_all(1 + 2 * step, c)
-        local[chunk(c), :] = local[chunk(c), :] + mm(picked, picked_w[...])
-
     for c in range(CHUNKS):
         res[chunk(c), :] = res[chunk(c), :] + receive(0, c)
         begin(0, c)
@@ -285,35 +360,42 @@
     rho = 1.0 / sigma
     for step in range(ITERS):
         stage = 1 + 2 * step
+        local[...] = mm(operand[...], inverse_w[...])
         for c in range(CHUNKS):
             finish(step, c)
+        local[...] = local[...] + mm(picks[...], picked_w[...])
         if step > 0:
             rho_new = 1.0 / (2.0 * sigma - rho)
             keep, gain = rho_new * rho, 2.0 * rho_new / spread
             rho = rho_new
+        relay_all(stage)
         for c in range(CHUNKS):
             update = local[chunk(c), :] + receive(stage, c)
             if step == 0:
                 moved = update / centre
-                sol[chunk(c), :] = moved
             else:
                 moved = keep * direction[chunk(c), :] + gain * update
-                sol[chunk(c), :] = sol[chunk(c), :] + moved
             direction[chunk(c), :] = moved
             rounded = moved.astype(bf16)
+            operand[chunk(c), :] = rounded
             pack(stage + 1, c, mm(rounded, schur_g[...]))
             send_all(stage + 1, c)
-            local[chunk(c), :] = mm(rounded, schur_w[...])
+        local[...] = mm(operand[...], schur_w[...])
+        if step == 0:
+            sol[...] = direction[...]
+        else:
+            sol[...] = sol[...] + direction[...]
         if step + 1 == ITERS:
             for at in range(width // LANES):
                 sol_out[0, 0, :, at * LANES:(at + 1) * LANES] = sol[at * LANES:(at + 1) * LANES, :].T
+        relay_all(stage + 1)
         for c in range(CHUNKS):
             res[chunk(c), :] = res[chunk(c), :] - (local[chunk(c), :] + receive(stage + 1, c))
             if step + 1 < ITERS:
                 begin(step + 1, c)
-    for at in range(width // LANES):
-        res_out[0, 0, :, at * LANES:(at + 1) * LANES] = res[at * LANES:(at + 1) * LANES, :].T
-
+            elif (c + 1) * wide % LANES == 0:
+                at = (c + 1) * wide // LANES - 1
+                res_out[0, 0, :, at * LANES:(at + 1) * LANES] = res[at * LANES:(at + 1) * LANES, :].T
     for copy in map_copies + coarse_copies:
         copy.wait_send()
     for at, s in enumerate(ring):
@@ -322,6 +404,16 @@
             send_sem=prim_send.at[at], recv_sem=prim_recv.at[0, 0, 0],
             device_id=ring_peer(s), device_id_type=MESH,
         ).wait_send()
+    for a in (-1, 0, 1):
+        ways = sum(a in chosen for chosen in RELAYED)
+
+        @pl.when((ways > 0) & ((me_y == 0) | (me_y == ny - 1)) & (me_x + a >= 0) & (me_x + a < nx))
+        def _(a=a):
+            pltpu.make_async_remote_copy(
+                src_ref=relay_buf.at[a + 1, :, pl.ds(0, ways)], dst_ref=relay_buf.at[a + 1, :, pl.ds(0, ways)],
+                send_sem=relay_send.at[a + 1], recv_sem=relay_recv.at[a + 1, 0, 0],
+                device_id=(me_x, turn), device_id_type=MESH,
+            ).wait_send()
     for d in range(8):
         @pl.when(inside(d))
         def _(d=d):
@@ -330,6 +422,14 @@
                 send_sem=out_send.at[d], recv_sem=out_recv.at[0, 0, 0],
                 device_id=peer(d), device_id_type=MESH,
             ).wait_send()
+
+
+def deliver(sol, res, sol_out, res_out, sems):
+    copies = [pltpu.make_async_copy(sol, sol_out, sems.at[0]), pltpu.make_async_copy(res, res_out, sems.at[1])]
+    for copy in copies:
+        copy.start()
+    for copy in copies:
+        copy.wait()
 
 
 def solution(mesh):
@@ -345,9 +445,10 @@
         smem = pl.BlockSpec(memory_space=pltpu.SMEM)
         dma = pltpu.SemaphoreType.DMA
         shape = jax.ShapeDtypeStruct(source.shape, f32)
-        return pl.pallas_call(
+        held = pltpu.VMEM(source.shape, f32)
+        results = pl.pallas_call(
             functools.partial(kernel, nx, ny),
-            out_shape=(shape, shape),
+            out_shape=(held, held),
             in_specs=[hbm, hbm, hbm, vmem, vmem, vmem, smem, vmem],
             out_specs=(vmem, vmem),
             scratch_shapes=[
@@ -370,23 +471,36 @@
                 pltpu.VMEM((width, rows), f32),
                 pltpu.VMEM((width, rows), f32),
                 pltpu.VMEM((width, slots), f32),
+                pltpu.VMEM((width, rows), bf16),
+                pltpu.VMEM((width, LANES), bf16),
                 pltpu.VMEM((8, stages, CHUNKS, half, LANES), f32),
                 pltpu.VMEM((8, stages, CHUNKS, half, LANES), f32),
+                pltpu.VMEM((3, stages, CHUNKS, half, LANES), f32),
                 pltpu.VMEM((links + 1, ITERS, CHUNKS, quarter, LANES), f32),
                 pltpu.VMEM((links, 1, modes), jnp.int32),
                 pltpu.VMEM((links, block, block), f32),
                 dma((3,)),
                 dma((8,)),
-                dma((stages, CHUNKS, 8)),
+                dma((2, CHUNKS, 8)),
+                dma((3,)),
+                dma((3, 2, CHUNKS)),
                 dma((links,)),
                 dma((ITERS, CHUNKS, links)),
                 dma((2, links)),
                 dma((2, links)),
             ],
             compiler_params=pltpu.CompilerParams(
-                collective_id=0, has_side_effects=True, vmem_limit_bytes=56 * 1024 * 1024
+                collective_id=0, has_side_effects=True, vmem_limit_bytes=62 * 1024 * 1024
             ),
         )(source, schur, inverse, jnp.swapaxes(basis, 2, 3), coarse, pmap[:, :, None, :], counts, order)
+        return pl.pallas_call(
+            deliver,
+            out_shape=(shape, shape),
+            in_specs=[vmem, vmem],
+            out_specs=(hbm, hbm),
+            scratch_shapes=[dma((2,))],
+            compiler_params=pltpu.CompilerParams(vmem_limit_bytes=1024 * 1024),
+        )(*[pltpu.with_memory_space_constraint(value, pltpu.VMEM) for value in results])
 
     placed = (P("sx", "sy", None, None),) * 5 + (P("sx", "sy", None),) * 3
     return jax.shard_map(

time: 81.4 us -> 69.7 us (0.86)
  Pallas kernels: 77.1 us -> 68.4 us
  local copies, waits for them, and re-layouts: 3.02 us -> 0 us
    pallas_call x1 -> x2, Pallas kernels: 77.1 us -> 68.4 us  [the longest x1 67.3 us: body(): pl.pallas_call(functools.partial(kernel, nx, ny), out_shape=(held, held),...]
    unnamed x4 -> x0, local copies, waits for them, and re-layouts: 3.02 us -> none
where the time goes in v2:
time: 69.7 us; the launch traced here: 69.2 us
  Pallas kernels  68.4 us (98%)
  between operations  0.8 us (1%)
    pallas_call x1, Pallas kernels, body(): pl.pallas_call(functools.partial(kernel, nx, ny), out_shape=(held, held),...  67.3 us

profile of v2, /device:TPU:13, one launch (start us, length us, event | category | flops | bytes accessed | tf_op | source)
XLA Modules:
  0.0 69.2 jit_solution(13300588772483899271)
XLA Ops:
  0.6 67.3 %shard_map.95 = (f32[1,1,768,256]{3,2,1,0:T(8,128)S(1)}, f32[1,1,768,256]{3,2,1,0:T(8,128)S(1)}) custom-call(f32[1,1,768,256]{3,2,1,0:T(8,128)} %source.1, bf16[1,1,768,768]{3,2,1,0:T(8,128)(2,1)} %schur.1, bf16[1,1,768,768]{3,2,1,0:T(8,128)(2,1)} %inverse.1, bf16[1,1,32,768]{3,2,1,0:T(8,128)(2,1)} %bitcast.2, f32[1,1,32,32]{3,2,1,0:T(8,128)} %coarse.1, ...), custom_call_target="tpu_custom_call" | custom-call | tf_op jit(solution)/shard_map/pallas_call | solution.py:449
  67.9 1.2 %shard_map.96 = (f32[1,1,768,256]{3,2,1,0:T(8,128)}, f32[1,1,768,256]{3,2,1,0:T(8,128)}) custom-call(f32[1,1,768,256]{3,2,1,0:T(8,128)S(1)} %get-tuple-element.4.sol, f32[1,1,768,256]{3,2,1,0:T(8,128)S(1)} %get-tuple-element.5.res), custom_call_target="tpu_custom_call" | custom-call | tf_op jit(solution)/shard_map/pallas_call | solution.py:496

commit v3 on v2

--- a/solution.py
+++ b/solution.py
@@ -10,7 +10,7 @@
 MROW = 64
 ITERS = 3
 CHUNKS = 4
-RELAYED = ((), (-1, 0, 1), (0,), ())
+RELAYED = (((), (-1, 0, 1), (-1, 0, 1), ()), ((), (-1, 0, 1), (-1, 0, 1), ()))
 LANES = 128
 MESH = pl.DeviceIdType.MESH
 
@@ -99,15 +99,17 @@
     for s in ring:
         pl.semaphore_signal(barrier, inc=1, device_id=ring_peer(s), device_id_type=MESH)
 
+    partner = me_x + 1 - 2 * lax.rem(me_x, 2)
     turn = ny // 2
     paired = {turn - 1: (ny - 1, 0), ny - 1: (turn - 1, turn), turn: (0, ny - 1), 0: (turn, turn - 1)}
     for mine, (straight, fan) in paired.items():
         at = me_y == mine
-        total = total + at.astype(jnp.int32)
+        total = total + 2 * at.astype(jnp.int32)
 
         @pl.when(at)
         def _(straight=straight):
-            pl.semaphore_signal(barrier, inc=1, device_id=(me_x, straight), device_id_type=MESH)
+            for x in (me_x, partner):
+                pl.semaphore_signal(barrier, inc=1, device_id=(x, straight), device_id_type=MESH)
 
         for a in (-1, 0, 1):
             valid = at & (me_x + a >= 0) & (me_x + a < nx)
@@ -171,17 +173,17 @@
         for d in send_order:
             a, b = directions[d]
             direct = inside(d)
-            if a in RELAYED[c] and b != 0:
+            if a in RELAYED[stage % 2][c] and b != 0:
                 crossing = me_y == (turn - 1 if b > 0 else turn)
 
                 @pl.when(inside(d) & crossing)
                 def _(d=d, a=a, b=b):
                     pltpu.make_async_remote_copy(
                         src_ref=out_buf.at[d, stage, c],
-                        dst_ref=relay_buf.at[a + 1, stage, c],
+                        dst_ref=relay_buf.at[a + 1, stage * CHUNKS + c],
                         send_sem=out_send.at[d],
                         recv_sem=relay_recv.at[a + 1, stage % 2, c],
-                        device_id=(me_x, ny - 1 if b > 0 else 0),
+                        device_id=(partner if a == 0 else me_x, ny - 1 if b > 0 else 0),
                         device_id_type=MESH,
                     ).start()
 
@@ -192,29 +194,31 @@
                 out_copy(stage, c, d).start()
 
     def relay(stage, c):
-        if not RELAYED[c]:
+        if not RELAYED[stage % 2][c]:
             return
         for b in (1, -1):
             @pl.when(me_y == (ny - 1 if b > 0 else 0))
             def _(b=b):
-                for a in RELAYED[c]:
-                    @pl.when((me_x + a >= 0) & (me_x + a < nx))
-                    def _(a=a):
+                for a in RELAYED[stage % 2][c]:
+                    home = partner if a == 0 else me_x
+
+                    @pl.when((home + a >= 0) & (home + a < nx))
+                    def _(a=a, home=home):
                         slot = 7 - directions.index((a, b))
                         pltpu.make_async_remote_copy(
-                            src_ref=relay_buf.at[a + 1, stage, c],
-                            dst_ref=relay_buf.at[a + 1, stage, c],
+                            src_ref=relay_buf.at[a + 1, stage * CHUNKS + c],
+                            dst_ref=relay_buf.at[a + 1, stage * CHUNKS + c],
                             send_sem=relay_send.at[a + 1],
                             recv_sem=relay_recv.at[a + 1, stage % 2, c],
-                            device_id=(me_x, turn - 1 if b > 0 else turn),
+                            device_id=(home, turn - 1 if b > 0 else turn),
                             device_id_type=MESH,
                         ).wait_recv()
                         pltpu.make_async_remote_copy(
-                            src_ref=relay_buf.at[a + 1, stage, c],
+                            src_ref=relay_buf.at[a + 1, stage * CHUNKS + c],
                             dst_ref=in_buf.at[slot, stage, c],
                             send_sem=relay_send.at[a + 1],
                             recv_sem=out_recv.at[stage % 2, c, slot],
-                            device_id=(me_x + a, turn if b > 0 else turn - 1),
+                            device_id=(home + a, turn if b > 0 else turn - 1),
                             device_id_type=MESH,
                         ).start()
 
@@ -289,7 +293,6 @@
     basis_q[...] = jnp.concatenate([basis_t.astype(f32)] * parts, axis=0).T.astype(bf16)
     picked_g[...] = jnp.concatenate([mm(basis_t, halved)] * parts, axis=0).astype(bf16)
     picked_w[...] = jnp.concatenate([basis_t.astype(f32) * scale] * parts, axis=0).astype(bf16)
-    relay_all(0)
     load_inverse.wait()
     inverse_w[...] = inverse_v[...].T
     inverse_g[...] = mm(inverse_w[...], halved).astype(bf16)
@@ -328,6 +331,7 @@
     schur_w[...] = schur_v[...].T
     schur_g[...] = mm(schur_w[...], scatter[...]).astype(bf16)
 
+    relay_all(0)
     for copy in map_copies + coarse_copies:
         copy.wait_recv()
 
@@ -360,10 +364,9 @@
     rho = 1.0 / sigma
     for step in range(ITERS):
         stage = 1 + 2 * step
-        local[...] = mm(operand[...], inverse_w[...])
         for c in range(CHUNKS):
             finish(step, c)
-        local[...] = local[...] + mm(picks[...], picked_w[...])
+        local[...] = mm(operand[...], inverse_w[...]) + mm(picks[...], picked_w[...])
         if step > 0:
             rho_new = 1.0 / (2.0 * sigma - rho)
             keep, gain = rho_new * rho, 2.0 * rho_new / spread
@@ -405,12 +408,12 @@
             device_id=ring_peer(s), device_id_type=MESH,
         ).wait_send()
     for a in (-1, 0, 1):
-        ways = sum(a in chosen for chosen in RELAYED)
+        ways = sum(a in chosen for stage in range(stages) for chosen in RELAYED[stage % 2])
 
         @pl.when((ways > 0) & ((me_y == 0) | (me_y == ny - 1)) & (me_x + a >= 0) & (me_x + a < nx))
         def _(a=a):
             pltpu.make_async_remote_copy(
-                src_ref=relay_buf.at[a + 1, :, pl.ds(0, ways)], dst_ref=relay_buf.at[a + 1, :, pl.ds(0, ways)],
+                src_ref=relay_buf.at[a + 1, pl.ds(0, ways)], dst_ref=relay_buf.at[a + 1, pl.ds(0, ways)],
                 send_sem=relay_send.at[a + 1], recv_sem=relay_recv.at[a + 1, 0, 0],
                 device_id=(me_x, turn), device_id_type=MESH,
             ).wait_send()
@@ -475,7 +478,7 @@
                 pltpu.VMEM((width, LANES), bf16),
                 pltpu.VMEM((8, stages, CHUNKS, half, LANES), f32),
                 pltpu.VMEM((8, stages, CHUNKS, half, LANES), f32),
-                pltpu.VMEM((3, stages, CHUNKS, half, LANES), f32),
+                pltpu.VMEM((3, stages * CHUNKS, half, LANES), f32),
                 pltpu.VMEM((links + 1, ITERS, CHUNKS, quarter, LANES), f32),
                 pltpu.VMEM((links, 1, modes), jnp.int32),
                 pltpu.VMEM((links, block, block), f32),

time: 69.7 us -> 67.3 us (0.966)
  Pallas kernels: 68.4 us -> 66.2 us
    pallas_call x1, Pallas kernels: 67.3 us -> 65 us  [body(): pl.pallas_call(functools.partial(kernel, nx, ny), out_shape=(held, held),...]
where the time goes in v3:
time: 67.3 us; the launch traced here: 67 us
  Pallas kernels  66.2 us (98%)
  between operations  0.8 us (1%)
    pallas_call x1, Pallas kernels, body(): pl.pallas_call(functools.partial(kernel, nx, ny), out_shape=(held, held),...  65 us

profile of v3, /device:TPU:13, one launch (start us, length us, event | category | flops | bytes accessed | tf_op | source)
XLA Modules:
  0.0 67.0 jit_solution(6142968146505653849)
XLA Ops:
  0.6 65.0 %shard_map.95 = (f32[1,1,768,256]{3,2,1,0:T(8,128)S(1)}, f32[1,1,768,256]{3,2,1,0:T(8,128)S(1)}) custom-call(f32[1,1,768,256]{3,2,1,0:T(8,128)} %source.1, bf16[1,1,768,768]{3,2,1,0:T(8,128)(2,1)} %schur.1, bf16[1,1,768,768]{3,2,1,0:T(8,128)(2,1)} %inverse.1, bf16[1,1,32,768]{3,2,1,0:T(8,128)(2,1)} %bitcast.2, f32[1,1,32,32]{3,2,1,0:T(8,128)} %coarse.1, ...), custom_call_target="tpu_custom_call" | custom-call | tf_op jit(solution)/shard_map/pallas_call | solution.py:452
  65.7 1.2 %shard_map.96 = (f32[1,1,768,256]{3,2,1,0:T(8,128)}, f32[1,1,768,256]{3,2,1,0:T(8,128)}) custom-call(f32[1,1,768,256]{3,2,1,0:T(8,128)S(1)} %get-tuple-element.4.sol, f32[1,1,768,256]{3,2,1,0:T(8,128)S(1)} %get-tuple-element.5.res), custom_call_target="tpu_custom_call" | custom-call | tf_op jit(solution)/shard_map/pallas_call | solution.py:499

commit v4 on v3

--- a/solution.py
+++ b/solution.py
@@ -10,7 +10,8 @@
 MROW = 64
 ITERS = 3
 CHUNKS = 4
-RELAYED = (((), (-1, 0, 1), (-1, 0, 1), ()), ((), (-1, 0, 1), (-1, 0, 1), ()))
+RELAYED = (((), (-1, 1), (-1, 0, 1), (0,)), ((), (-1, 1), (-1, 0, 1), (0,)))
+FORWARDS = ((1, 2), (3,), (), ())
 LANES = 128
 MESH = pl.DeviceIdType.MESH
 
@@ -233,6 +234,10 @@
         for c in range(CHUNKS):
             relay(stage, c)
 
+    def forward(stage, place):
+        for c in FORWARDS[place]:
+            relay(stage, c)
+
     def receive(stage, c):
         wait_all(stage, c)
         tops, lows = [], []
@@ -254,8 +259,8 @@
 
     def prim_copies(step, c):
         return ring_copies(
-            prim_buf.at[links, step, c], lambda t: prim_buf.at[t, step, c],
-            lambda t: prim_send.at[t], lambda t: prim_recv.at[step, c, t],
+            prim_buf.at[step, c, links], lambda t: prim_buf.at[step, c, t],
+            lambda t: prim_send.at[t], lambda t: prim_recv.at[step, c],
         )
 
     def chunk(c):
@@ -305,19 +310,22 @@
         packed = primal[:quarter]
         for q in range(1, parts):
             packed = jnp.where(part_of == q, primal[q * quarter:(q + 1) * quarter], packed)
-        prim_buf[links, step, c] = packed
+        prim_buf[step, c, links] = packed
         for copy in prim_copies(step, c):
             copy.start()
         shared[chunk(c), :] = mm(scaled, inverse_g[...])
         operand[chunk(c), :] = scaled
 
     def wait_prim(step, c):
-        for copy in prim_copies(step, c):
-            copy.wait_recv()
+        arrived = prim_buf.at[step, c, pl.ds(0, links)]
+        pltpu.make_async_remote_copy(
+            src_ref=arrived, dst_ref=arrived, send_sem=prim_send.at[0], recv_sem=prim_recv.at[step, c],
+            device_id=ring_peer(1), device_id_type=MESH,
+        ).wait_recv()
 
     def finish(step, c):
         wait_prim(step, c)
-        primal = jnp.concatenate([prim_buf[t, step, c] for t in range(links + 1)], axis=1)
+        primal = jnp.concatenate([prim_buf[step, c, t] for t in range(links + 1)], axis=1)
         both = mm(jnp.concatenate(split(primal), axis=0), cmat[...])
         packed = both[:quarter, :LANES] + (both[quarter:, :LANES] + both[:quarter, LANES:])
         picked = jnp.concatenate(
@@ -371,8 +379,8 @@
             rho_new = 1.0 / (2.0 * sigma - rho)
             keep, gain = rho_new * rho, 2.0 * rho_new / spread
             rho = rho_new
-        relay_all(stage)
         for c in range(CHUNKS):
+            forward(stage, c)
             update = local[chunk(c), :] + receive(stage, c)
             if step == 0:
                 moved = update / centre
@@ -391,8 +399,8 @@
         if step + 1 == ITERS:
             for at in range(width // LANES):
                 sol_out[0, 0, :, at * LANES:(at + 1) * LANES] = sol[at * LANES:(at + 1) * LANES, :].T
-        relay_all(stage + 1)
         for c in range(CHUNKS):
+            forward(stage + 1, c)
             res[chunk(c), :] = res[chunk(c), :] - (local[chunk(c), :] + receive(stage + 1, c))
             if step + 1 < ITERS:
                 begin(step + 1, c)
@@ -403,8 +411,8 @@
         copy.wait_send()
     for at, s in enumerate(ring):
         pltpu.make_async_remote_copy(
-            src_ref=prim_buf.at[links], dst_ref=prim_buf.at[links - 1 - at],
-            send_sem=prim_send.at[at], recv_sem=prim_recv.at[0, 0, 0],
+            src_ref=prim_buf.at[:, :, links], dst_ref=prim_buf.at[:, :, links - 1 - at],
+            send_sem=prim_send.at[at], recv_sem=prim_recv.at[0, 0],
             device_id=ring_peer(s), device_id_type=MESH,
         ).wait_send()
     for a in (-1, 0, 1):
@@ -479,7 +487,7 @@
                 pltpu.VMEM((8, stages, CHUNKS, half, LANES), f32),
                 pltpu.VMEM((8, stages, CHUNKS, half, LANES), f32),
                 pltpu.VMEM((3, stages * CHUNKS, half, LANES), f32),
-                pltpu.VMEM((links + 1, ITERS, CHUNKS, quarter, LANES), f32),
+                pltpu.VMEM((ITERS, CHUNKS, links + 1, quarter, LANES), f32),
                 pltpu.VMEM((links, 1, modes), jnp.int32),
                 pltpu.VMEM((links, block, block), f32),
                 dma((3,)),
@@ -488,7 +496,7 @@
                 dma((3,)),
                 dma((3, 2, CHUNKS)),
                 dma((links,)),
-                dma((ITERS, CHUNKS, links)),
+                dma((ITERS, CHUNKS)),
                 dma((2, links)),
                 dma((2, links)),
             ],

time: 67.3 us -> 66.6 us (0.990)
  Pallas kernels: 66.2 us -> 64.8 us
    pallas_call x1, Pallas kernels: 65 us -> 63.7 us  [body(): pl.pallas_call(functools.partial(kernel, nx, ny), out_shape=(held, held),...]
where the time goes in v4:
time: 66.6 us; the launch traced here: 65.6 us
  Pallas kernels  64.8 us (97%)
  between operations  0.8 us (1%)
    pallas_call x1, Pallas kernels, body(): pl.pallas_call(functools.partial(kernel, nx, ny), out_shape=(held, held),...  63.7 us

profile of v4, /device:TPU:13, one launch (start us, length us, event | category | flops | bytes accessed | tf_op | source)
XLA Modules:
  0.0 65.6 jit_solution(12555171790847455721)
XLA Ops:
  0.6 63.7 %shard_map.95 = (f32[1,1,768,256]{3,2,1,0:T(8,128)S(1)}, f32[1,1,768,256]{3,2,1,0:T(8,128)S(1)}) custom-call(f32[1,1,768,256]{3,2,1,0:T(8,128)} %source.1, bf16[1,1,768,768]{3,2,1,0:T(8,128)(2,1)} %schur.1, bf16[1,1,768,768]{3,2,1,0:T(8,128)(2,1)} %inverse.1, bf16[1,1,32,768]{3,2,1,0:T(8,128)(2,1)} %bitcast.2, f32[1,1,32,32]{3,2,1,0:T(8,128)} %coarse.1, ...), custom_call_target="tpu_custom_call" | custom-call | tf_op jit(solution)/shard_map/pallas_call | solution.py:460
  64.3 1.2 %shard_map.96 = (f32[1,1,768,256]{3,2,1,0:T(8,128)}, f32[1,1,768,256]{3,2,1,0:T(8,128)}) custom-call(f32[1,1,768,256]{3,2,1,0:T(8,128)S(1)} %get-tuple-element.4.sol, f32[1,1,768,256]{3,2,1,0:T(8,128)S(1)} %get-tuple-element.5.res), custom_call_target="tpu_custom_call" | custom-call | tf_op jit(solution)/shard_map/pallas_call | solution.py:507
